TPU v7x, 512 devices: a whole 4x4x16 slice. The times are simulated.
512 devices in a mesh: dp: 16 (over z), pipe: 4 (over x), tensor: 8 (over y, core).
Axes of the slice: x: 4, y: 4, z: 16, core: 2. Of those that a mesh axis runs over, the one named last changes fastest.
Arguments:
- tokens: bfloat16 [16384, 8192], P('dp', ('pipe', 'tensor')), may hold values from -6 to 6
- key_value_weight: bfloat16 [8192, 2048], P(('pipe', 'tensor')), may hold values from -0.0625 to 0.0625
- adapter_down: bfloat16 [96, 8192, 128], P(None, ('pipe', 'tensor', 'dp')), may hold values from -0.0625 to 0.0625
- adapter_up: bfloat16 [96, 64, 2048], P(None, 'dp'), may hold values from -0.75 to 0.75
- tenant_of_block: int32 [128], replicated, may hold values from 0 to 95
- slot_of_tenant: int32 [96], replicated, may hold values from 0 to 95, each once
- cotangent: bfloat16 [16384, 2048], P(('dp', 'pipe', 'tensor')), may hold values from -1.5 to 1.5
Outputs:
- key_value: bfloat16 [16384, 2048], P(('dp', 'pipe', 'tensor'))
- input_grad: bfloat16 [16384, 8192], P('dp', ('pipe', 'tensor'))
- grad_a: float32 [96, 8192, 128], P(None, ('pipe', 'tensor', 'dp'))
- grad_b: float32 [96, 64, 2048], P(None, 'dp', ('pipe', 'tensor'))
Inputs may be any that keep to these rules, and one draw needn't show every extreme that they name: `slot_of_tenant`: each slot holds exactly one tenant.
All inputs are finite; a program needn't handle non-finite values.
Results may differ from a plain program's by a relative error of at most 0.017.
Values may be sent and summed in bfloat16 or wider, within the bound.
A program may use at most 64 MiB of HBM per device.

v0:
```python
import jax
import jax.numpy as jnp
from jax import lax
from jax.sharding import PartitionSpec as P

KEY_WIDTH = 1024
ADAPTER_RANK = 64
BLOCK = 128


def body(
    tokens, key_value_weight, adapter_down, adapter_up, tenant_of_block, slot_of_tenant, cotangent
):
    data_count = lax.axis_size("dp")
    group_count = lax.axis_size(("pipe", "tensor"))
    my_group = lax.axis_index(("pipe", "tensor"))
    tok_dev, feature_count = tokens.shape
    blocks_dev = tok_dev // BLOCK
    row_count = tok_dev // group_count
    tenant_list = slot_of_tenant.shape[0]
    all_blocks = tenant_of_block.shape[0]
    tenant_ids = lax.broadcasted_iota(jnp.int32, (all_blocks, tenant_list), 1)
    slot_of_block = jnp.sum(
        jnp.where(tenant_of_block[:, None] == tenant_ids, slot_of_tenant[None, :], 0), axis=1
    )
    slot_match = slot_of_block[:, None] == tenant_ids
    down_rows = adapter_down.shape[1]
    a_send = jnp.dot(
        slot_match.astype(jnp.bfloat16),
        adapter_down.reshape(tenant_list, down_rows * 2 * ADAPTER_RANK),
        preferred_element_type=jnp.float32,
    )
    a_send = a_send.astype(jnp.bfloat16).reshape(all_blocks, down_rows, 2 * ADAPTER_RANK)
    own_block = my_group * row_count // BLOCK
    own_slots = lax.dynamic_index_in_dim(
        slot_of_block.reshape(data_count, blocks_dev), own_block, 1, False
    )
    owner_choice = (
        own_slots[:, None] == lax.broadcasted_iota(jnp.int32, (data_count, tenant_list), 1)
    ).astype(jnp.bfloat16)
    up_rows = adapter_up.shape[1]
    b_send = jnp.dot(
        owner_choice,
        adapter_up.reshape(tenant_list, up_rows * 2 * KEY_WIDTH),
        preferred_element_type=jnp.float32,
    )
    b_send = b_send.astype(jnp.bfloat16).reshape(data_count, up_rows, 2 * KEY_WIDTH)
    down_blocks, b_own = (
        lax.all_to_all(a_send, "dp", split_axis=0, concat_axis=1, tiled=True),
        lax.all_to_all(b_send, "dp", split_axis=0, concat_axis=1, tiled=True),
    )
    b_own = b_own[0]
    tok_blocks = tokens.reshape(blocks_dev, BLOCK, feature_count)
    low_part = jnp.einsum(
        "bif,bfr->bir", tok_blocks, down_blocks, preferred_element_type=jnp.float32
    ).reshape(tok_dev, 2 * ADAPTER_RANK)
    low_all = lax.psum(low_part.astype(jnp.bfloat16), ("pipe", "tensor"))
    base_out = lax.psum_scatter(
        jnp.dot(tokens, key_value_weight, preferred_element_type=jnp.float32).astype(jnp.bfloat16),
        ("pipe", "tensor"),
        scatter_dimension=0,
        tiled=True,
    ).astype(jnp.float32)
    low_rows = lax.dynamic_slice_in_dim(low_all, my_group * row_count, row_count, 0)
    lowrank = jnp.concatenate(
        [
            jnp.dot(
                low_rows[:, :ADAPTER_RANK], b_own[:, :KEY_WIDTH], preferred_element_type=jnp.float32
            ),
            jnp.dot(
                low_rows[:, ADAPTER_RANK:], b_own[:, KEY_WIDTH:], preferred_element_type=jnp.float32
            ),
        ],
        axis=1,
    )
    key_value = (base_out + lowrank).astype(jnp.bfloat16)
    contract_last = (((1,), (1,)), ((), ()))
    grad_rows = jnp.concatenate(
        [
            lax.dot_general(
                cotangent[:, :KEY_WIDTH],
                b_own[:, :KEY_WIDTH],
                contract_last,
                preferred_element_type=jnp.float32,
            ),
            lax.dot_general(
                cotangent[:, KEY_WIDTH:],
                b_own[:, KEY_WIDTH:],
                contract_last,
                preferred_element_type=jnp.float32,
            ),
        ],
        axis=1,
    )
    grad_rows = grad_rows.astype(jnp.bfloat16)
    cot_all, grad_low = (
        lax.all_gather(cotangent, ("pipe", "tensor"), axis=0, tiled=True),
        lax.all_gather(grad_rows, ("pipe", "tensor"), axis=0, tiled=True),
    )
    grad_blocks = grad_low.reshape(blocks_dev, BLOCK, 2 * ADAPTER_RANK)
    input_grad = lax.dot_general(
        cot_all, key_value_weight, contract_last, preferred_element_type=jnp.float32
    )
    input_grad = input_grad + jnp.einsum(
        "bir,bfr->bif", grad_blocks, down_blocks, preferred_element_type=jnp.float32
    ).reshape(tok_dev, feature_count)
    input_grad = input_grad.astype(jnp.bfloat16)
    grad_a_part = jnp.einsum(
        "bif,bir->bfr", tok_blocks, grad_blocks, preferred_element_type=jnp.float32
    )
    col_count = 2 * KEY_WIDTH // group_count
    col_start = my_group * col_count
    half_index = col_start // KEY_WIDTH
    low_half = lax.dynamic_slice_in_dim(
        low_all, half_index * ADAPTER_RANK, ADAPTER_RANK, 1
    ).reshape(blocks_dev, BLOCK, ADAPTER_RANK)
    cot_cols = lax.dynamic_slice_in_dim(cot_all, col_start, col_count, 1).reshape(
        blocks_dev, BLOCK, col_count
    )
    grad_b_part = jnp.einsum("bir,bic->brc", low_half, cot_cols, preferred_element_type=jnp.float32)
    grad_a_recv, grad_b_recv = (
        lax.all_to_all(
            grad_a_part.astype(jnp.bfloat16), "dp", split_axis=1, concat_axis=0, tiled=True
        ).astype(grad_a_part.dtype),
        lax.all_to_all(
            grad_b_part.astype(jnp.bfloat16), "dp", split_axis=1, concat_axis=0, tiled=True
        ).astype(grad_b_part.dtype),
    )
    slot_weight = slot_match.astype(jnp.float32)
    grad_a = jnp.einsum(
        "bt,bx->tx",
        slot_weight,
        grad_a_recv.reshape(all_blocks, down_rows * 2 * ADAPTER_RANK),
        precision=lax.Precision.HIGHEST,
    )
    grad_a = grad_a.reshape(tenant_list, down_rows, 2 * ADAPTER_RANK)
    grad_b = jnp.einsum(
        "bt,bx->tx",
        slot_weight,
        grad_b_recv.reshape(all_blocks, grad_b_recv.shape[1] * col_count),
        precision=lax.Precision.HIGHEST,
    )
    grad_b = grad_b.reshape(tenant_list, grad_b_recv.shape[1], col_count)
    return (key_value, input_grad, grad_a, grad_b)


def solution(mesh):
    placed = (
        P("dp", ("pipe", "tensor")),
        P(("pipe", "tensor"), None),
        P(None, ("pipe", "tensor", "dp"), None),
        P(None, "dp", None),
        P(),
        P(),
        P(("dp", "pipe", "tensor"), None),
    )
    return jax.shard_map(
        body,
        mesh=mesh,
        in_specs=placed,
        out_specs=(
            P(("dp", "pipe", "tensor"), None),
            P("dp", ("pipe", "tensor")),
            P(None, ("pipe", "tensor", "dp"), None),
            P(None, "dp", ("pipe", "tensor")),
        ),
        check_vma=False,
    )
```

profile of v0, /device:TPU:2, one launch (start us, length us, event | category | flops | bytes accessed | tf_op | source)
XLA Modules:
  0.0 395.1 jit_solution(17106891758424243477)
XLA Ops:
  7.2 0.9 select_reduce_fusion
  8.1 1.3 fusion.2
  9.6 44.1 %all_to_all.57 = bf16[128,16,128]{2,1,0:T(8,128)(2,1)S(1)} all-to-all(bf16[128,16,128]{2,1,0:T(8,128)(2,1)S(1)} %bitcast.78), channel_id=1, replica_groups=mesh['dp'=16,'pipe'=4,'tensor'=8] {'dp'}, dimensions={0} | all-to-all | bytes 1048576 | tf_op jit(solution)/shard_map/all_to_all | solution.py:49
  53.7 0.8 copy-done.2
  54.8 0.9 copy.41
  55.7 3.2 convolution_convert_fusion.1
  59.8 2.4 copy.61
  63.0 24.5 %all_to_all.58 = bf16[16,4,2048]{2,1,0:T(4,128)(2,1)S(1)} all-to-all(bf16[16,4,2048]{2,1,0:T(4,128)(2,1)S(1)} %reshape.64), channel_id=1, replica_groups=mesh['dp'=16,'pipe'=4,'tensor'=8] {'dp'}, dimensions={0} | all-to-all | bytes 524288 | tf_op jit(solution)/shard_map/all_to_all | solution.py:50
  88.4 24.9 %all_gather.7 = bf16[1024,128]{1,0:T(8,128)(2,1)S(1)} all-gather(bf16[32,128]{1,0:T(8,128)(2,1)S(1)} %pad_maximum_fusion), channel_id=1, replica_groups=mesh['dp'=16,'pipe'=4,'tensor'=8] {'pipe','tensor'}, dimensions={0}, use_global_device_ids=true | all-gather | bytes 270336 | tf_op jit(solution)/shard_map/all_gather | solution.py:98
  113.6 1.1 copy.43
  114.7 5.8 %all-to-all-start.2 = ((bf16[8,256,128]{2,0,1:T(8,128)(2,1)}), bf16[8,256,128]{2,0,1:T(8,128)(2,1)S(1)}, u32[]{:S(2)}, u32[]{:S(2)}) async-start(bf16[8,256,128]{2,0,1:T(8,128)(2,1)} %copy.43), calls=%async_computation.3 | async-start | bytes 1048576 | tf_op jit(solution)/shard_map/all_to_all | solution.py:122
  120.8 63.9 %all-reduce.2.cloned.1.call-done = bf16[1024,128]{0,1:T(8,128)(2,1)} async-done(((bf16[1024,128]{0,1:T(8,128)(2,1)}), bf16[1024,128]{0,1:T(8,128)(2,1)}) %all-reduce.2.cloned.1.call-update) | async-done | bytes 262160 | tf_op jit(solution)/shard_map/psum | solution.py:57
  184.8 1.2 fusion.14
  185.9 1.2 fusion.11
  187.7 1.3 copy.53
  189.1 105.7 %reduce-scatter.2.cloned.1.call-done = bf16[32,2048]{1,0:T(8,128)(2,1)} async-done(((bf16[1024,2048]{1,0:T(8,128)(2,1)}), bf16[32,2048]{1,0:T(8,128)(2,1)}) %reduce-scatter.2.cloned.1.call-update) | async-done | bytes 131088 | tf_op jit(solution)/shard_map/reduce_scatter | solution.py:58
  294.8 1.6 fusion.7
  296.4 62.4 %all-gather.2.cloned.1.call-done = bf16[1024,2048]{1,0:T(8,128)(2,1)} async-done(((bf16[32,2048]{1,0:T(8,128)(2,1)}), bf16[1024,2048]{1,0:T(8,128)(2,1)}) %all-gather.2.cloned.1.call-update) | async-done | bytes 4194320 | tf_op jit(solution)/shard_map/all_gather | solution.py:97
  358.8 1.1 constant_dynamic-slice_fusion
  359.9 1.1 convolution_convert_fusion.5
  361.9 12.3 %all-to-all-start.3 = ((bf16[16,2,1024]{2,1,0:T(2,128)(2,1)}), bf16[16,2,1024]{2,1,0:T(2,128)(2,1)S(1)}, u32[]{:S(2)}, u32[]{:S(2)}) async-start(bf16[16,2,1024]{2,1,0:T(2,128)(2,1)} %reshape.73), calls=%async_computation.4 | async-start | bytes 131072 | tf_op jit(solution)/shard_map/all_to_all | solution.py:125
  374.2 4.3 %fusion = bf16[1024,256]{1,0:T(8,128)(2,1)} fusion(f32[1024,256]{1,0:T(8,128)S(1)} %bitcast.81, bf16[1024,2048]{1,0:T(8,128)(2,1)} %all-gather.2.cloned.1.call-done, bf16[256,2048]{1,0:T(8,128)(2,1)S(1)} %copy-done), kind=kOutput, calls=%fused_computation.4 | convolution fusion | flops 1074266112 | bytes 6815744 | tf_op jit(solution)/shard_map/dot_general | solution.py:101
  378.4 8.9 %all-to-all-done.3 = bf16[16,2,1024]{2,1,0:T(2,128)(2,1)S(1)} async-done(((bf16[16,2,1024]{2,1,0:T(2,128)(2,1)}), bf16[16,2,1024]{2,1,0:T(2,128)(2,1)S(1)}, u32[]{:S(2)}, u32[]{:S(2)}) %all-to-all-start.3) | async-done | bytes 65568 | tf_op jit(solution)/shard_map/all_to_all | solution.py:125
  387.8 0.8 fusion.19
  (39 shorter events, 5.5 us)
Async XLA Ops:
  7.2 48.6 %copy-start = (bf16[256,2048]{1,0:T(8,128)(2,1)S(1)}, bf16[256,2048]{1,0:T(8,128)(2,1)}, u32[]{:S(2)}) copy-start(bf16[256,2048]{1,0:T(8,128)(2,1)} %param.8) | copy-start | bytes 3145732
  7.2 47.3 %copy-start.1 = (bf16[1024,256]{1,0:T(8,128)(2,1)S(1)}, bf16[1024,256]{1,0:T(8,128)(2,1)}, u32[]{:S(2)}) copy-start(bf16[1024,256]{1,0:T(8,128)(2,1)} %param.7) | copy-start | bytes 1572868
  7.2 177.6 %all-reduce.2.cloned.1.call-start = ((), (), s32[]{:S(2)}) async-start(), calls=%async_computation.6 | async-start | bytes 524288 | tf_op jit(solution)/shard_map/psum | solution.py:57
  53.7 0.8 copy-start.2
  55.7 239.1 %reduce-scatter.2.cloned.1.call-start = ((), (), s32[]{:S(2)}) async-start(), calls=%async_computation.5 | async-start | bytes 4325376 | tf_op jit(solution)/shard_map/reduce_scatter | solution.py:58
  59.0 28.6 %copy-start.5 = (bf16[32,2048]{1,0:T(8,128)(2,1)S(1)}, bf16[32,2048]{1,0:T(8,128)(2,1)}, u32[]{:S(2)}) copy-start(bf16[32,2048]{1,0:T(8,128)(2,1)} %param.13) | copy-start | bytes 393220
  59.0 299.8 %all-gather.2.cloned.1.call-start = ((), (), s32[]{:S(2)}) async-start(), calls=%async_computation.7 | async-start | bytes 4325376 | tf_op jit(solution)/shard_map/all_gather | solution.py:97
  62.8 57.7 %copy-start.3 = (bf16[16,8,16,128]{3,2,0,1:T(8,128)(2,1)S(1)}, bf16[16,8,16,128]{3,2,0,1:T(8,128)(2,1)}, u32[]{:S(2)}) copy-start(bf16[16,8,16,128]{3,2,0,1:T(8,128)(2,1)} %copy-done.2) | copy-start | bytes 1572868
  87.6 0.7 copy-start.4
  114.7 72.4 %all-to-all-start.2 = ((bf16[8,256,128]{2,0,1:T(8,128)(2,1)}), bf16[8,256,128]{2,0,1:T(8,128)(2,1)S(1)}, u32[]{:S(2)}, u32[]{:S(2)}) async-start(bf16[8,256,128]{2,0,1:T(8,128)(2,1)} %copy.43), calls=%async_computation.3 | async-start | bytes 1048576 | tf_op jit(solution)/shard_map/all_to_all | solution.py:122
  361.9 25.5 %all-to-all-start.3 = ((bf16[16,2,1024]{2,1,0:T(2,128)(2,1)}), bf16[16,2,1024]{2,1,0:T(2,128)(2,1)S(1)}, u32[]{:S(2)}, u32[]{:S(2)}) async-start(bf16[16,2,1024]{2,1,0:T(2,128)(2,1)} %reshape.73), calls=%async_computation.4 | async-start | bytes 131072 | tf_op jit(solution)/shard_map/all_to_all | solution.py:125
Sparse Core Ops, SparseCore 0:
  55.8 128.9 all-reduce.1
  189.3 105.4 reduce-scatter.1
  297.9 60.8 all-gather.1
where the time goes:
time: 396 us; the launch traced here: 395 us
  waiting for transfers between devices  242 us (61%)
  blocking collectives  93.4 us (24%)
  starting transfers between devices  18.2 us (5%)
  matrix products  15 us (4%)
  between operations  14 us (4%)
  local copies, waits for them, and re-layouts  10.2 us (3%)
    reduce_scatter x1, waiting for transfers between devices, body(): lax.psum_scatter(jnp.dot(tokens, key_value_weight, preferred_element_type...  106 us
    psum x1, waiting for transfers between devices, body(): low_all = lax.psum(low_part.astype(jnp.bfloat16), ('pipe', 'tensor'))  63.9 us
    all_gather x1, waiting for transfers between devices, body(): lax.all_gather(cotangent, ('pipe', 'tensor'), axis=0, tiled=True)  62.4 us
    all_to_all x1, blocking collectives, body(): lax.all_to_all(a_send, 'dp', split_axis=0, concat_axis=1, tiled=True)  44.1 us
    all_gather x1, blocking collectives, body(): lax.all_gather(grad_rows, ('pipe', 'tensor'), axis=0, tiled=True)  24.9 us
    all_to_all x1, blocking collectives, body(): lax.all_to_all(b_send, 'dp', split_axis=0, concat_axis=1, tiled=True)  24.5 us
    all_to_all x1, starting transfers between devices, body(): lax.all_to_all(grad_b_part.astype(jnp.bfloat16), 'dp', split_axis=1, conc...  12.3 us
    all_to_all x1, waiting for transfers between devices, body(): lax.all_to_all(grad_b_part.astype(jnp.bfloat16), 'dp', split_axis=1, conc...  8.89 us
  transfers between devices with their start and end apart: 5, of which 4 were waited for; matrix products, arithmetic and copies ran while one was open for 5% of the time, Pallas kernels for 0%

commit v1 on v0

--- a/solution.py
+++ b/solution.py
@@ -54,7 +54,9 @@
     low_part = jnp.einsum(
         "bif,bfr->bir", tok_blocks, down_blocks, preferred_element_type=jnp.float32
     ).reshape(tok_dev, 2 * ADAPTER_RANK)
-    low_all = lax.psum(low_part.astype(jnp.bfloat16), ("pipe", "tensor"))
+    x = low_part.astype(jnp.bfloat16)
+    terms = lax.all_gather(x, ("pipe", "tensor"), axis=0, tiled=False)
+    low_all = terms.sum(axis=0)
     base_out = lax.psum_scatter(
         jnp.dot(tokens, key_value_weight, preferred_element_type=jnp.float32).astype(jnp.bfloat16),
         ("pipe", "tensor"),

time: 396 us -> 267 us (0.67)
  waiting for transfers between devices: 242 us -> 117 us
  starting transfers between devices: 18.2 us -> 12.5 us
  other arithmetic: 2.55 us -> 7.22 us
    psum x1 -> x0, waiting for transfers between devices: 63.9 us -> none  [body(): low_all = lax.psum(low_part.astype(jnp.bfloat16), ('pipe', 'tensor'))]
    all_gather x1, waiting for transfers between devices: 62.4 us -> 0.01 us  [body(): lax.all_gather(cotangent, ('pipe', 'tensor'), axis=0, tiled=True)]
    all_to_all x1, waiting for transfers between devices: 0.01 us -> 29 us  [body(): lax.all_to_all(grad_a_part.astype(jnp.bfloat16), 'dp', split_axis=1, conc...]
    reduce_scatter x1, waiting for transfers between devices: 106 us -> 87.5 us  [body(): lax.psum_scatter(jnp.dot(tokens, key_value_weight, preferred_element_type...]
    all_to_all x1, waiting for transfers between devices: 8.89 us -> 0.01 us  [body(): lax.all_to_all(grad_b_part.astype(jnp.bfloat16), 'dp', split_axis=1, conc...]
    all_to_all x1, starting transfers between devices: 12.3 us -> 6.58 us  [body(): lax.all_to_all(grad_b_part.astype(jnp.bfloat16), 'dp', split_axis=1, conc...]
    reduce_sum x0 -> x1, other arithmetic: none -> 4.79 us  [body(): low_all = terms.sum(axis=0)]
  transfers between devices with their start and end apart: 5 -> 5, of which waited for: 4 -> 2; matrix products, arithmetic and copies ran while one was open for 5% -> 10% of each run, Pallas kernels for 0% -> 0%
where the time goes in v1:
time: 267 us
  waiting for transfers between devices  117 us (44%)
  blocking collectives  93.4 us (35%)
  between operations  14 us (5%)
  matrix products  12.9 us (5%)
  starting transfers between devices  12.5 us (5%)
  local copies, waits for them, and re-layouts  9.53 us (4%)
  other arithmetic  7.22 us (3%)
    reduce_scatter x1, waiting for transfers between devices, body(): lax.psum_scatter(jnp.dot(tokens, key_value_weight, preferred_element_type...  87.5 us
    all_to_all x1, blocking collectives, body(): lax.all_to_all(a_send, 'dp', split_axis=0, concat_axis=1, tiled=True)  44.1 us
    all_to_all x1, waiting for transfers between devices, body(): lax.all_to_all(grad_a_part.astype(jnp.bfloat16), 'dp', split_axis=1, conc...  29 us
    all_gather x1, blocking collectives, body(): lax.all_gather(grad_rows, ('pipe', 'tensor'), axis=0, tiled=True)  24.9 us
    all_to_all x1, blocking collectives, body(): lax.all_to_all(b_send, 'dp', split_axis=0, concat_axis=1, tiled=True)  24.5 us
    all_to_all x1, starting transfers between devices, body(): lax.all_to_all(grad_b_part.astype(jnp.bfloat16), 'dp', split_axis=1, conc...  6.58 us
    unnamed x19, local copies, waits for them, and re-layouts  6.01 us
    all_to_all x1, starting transfers between devices, body(): lax.all_to_all(grad_a_part.astype(jnp.bfloat16), 'dp', split_axis=1, conc...  5.81 us
  transfers between devices with their start and end apart: 5, of which 2 were waited for; matrix products, arithmetic and copies ran while one was open for 10% of the time, Pallas kernels for 0%

profile of v1, /device:TPU:2, one launch (start us, length us, event | category | flops | bytes accessed | tf_op | source)
XLA Modules:
  0.0 266.7 jit_solution(2806579723638151195)
XLA Ops:
  7.2 0.7 all-gather.5.cloned.1.call-update
  8.0 0.8 select_reduce_fusion
  8.7 1.3 fusion.2
  10.2 44.1 %all_to_all.57 = bf16[128,16,128]{2,1,0:T(8,128)(2,1)S(1)} all-to-all(bf16[128,16,128]{2,1,0:T(8,128)(2,1)S(1)} %bitcast.73), channel_id=1, replica_groups=mesh['dp'=16,'pipe'=4,'tensor'=8] {'dp'}, dimensions={0} | all-to-all | bytes 1048576 | tf_op jit(solution)/shard_map/all_to_all | solution.py:49
  54.3 0.8 copy-done.2
  55.1 1.0 convolution_convert_fusion.4
  56.2 3.2 %convolution_convert_fusion.1 = bf16[1024,2048]{1,0:T(8,128)(2,1)} fusion(bf16[1024,256]{1,0:T(8,128)(2,1)S(1)} %copy-done.1, bf16[256,2048]{1,0:T(8,128)(2,1)S(1)} %copy-done), kind=kOutput, calls=%fused_computation.1 | convolution fusion | flops 1075838976 | bytes 5767168 | tf_op jit(solution)/shard_map/dot_general | solution.py:61
  59.5 2.4 copy.61
  62.1 0.4 convolution_convert_fusion
  62.7 24.5 %all_to_all.58 = bf16[16,4,2048]{2,1,0:T(4,128)(2,1)S(1)} all-to-all(bf16[16,4,2048]{2,1,0:T(4,128)(2,1)S(1)} %reshape.74), channel_id=1, replica_groups=mesh['dp'=16,'pipe'=4,'tensor'=8] {'dp'}, dimensions={0} | all-to-all | bytes 524288 | tf_op jit(solution)/shard_map/all_to_all | solution.py:50
  87.6 0.4 copy-done.4
  88.1 24.9 %all_gather.12 = bf16[1024,128]{1,0:T(8,128)(2,1)S(1)} all-gather(bf16[32,128]{1,0:T(8,128)(2,1)S(1)} %pad_maximum_fusion), channel_id=1, replica_groups=mesh['dp'=16,'pipe'=4,'tensor'=8] {'pipe','tensor'}, dimensions={0}, use_global_device_ids=true | all-gather | bytes 270336 | tf_op jit(solution)/shard_map/all_gather | solution.py:100
  113.3 1.1 copy.41
  114.4 5.8 %all-to-all-start.2 = ((bf16[8,256,128]{2,0,1:T(8,128)(2,1)}), bf16[8,256,128]{2,0,1:T(8,128)(2,1)S(1)}, u32[]{:S(2)}, u32[]{:S(2)}) async-start(bf16[8,256,128]{2,0,1:T(8,128)(2,1)} %copy.41), calls=%async_computation.3 | async-start | bytes 1048576 | tf_op jit(solution)/shard_map/all_to_all | solution.py:124
  120.5 29.0 %all-to-all-done.2 = bf16[8,256,128]{2,0,1:T(8,128)(2,1)S(1)} async-done(((bf16[8,256,128]{2,0,1:T(8,128)(2,1)}), bf16[8,256,128]{2,0,1:T(8,128)(2,1)S(1)}, u32[]{:S(2)}, u32[]{:S(2)}) %all-to-all-start.2) | async-done | bytes 524320 | tf_op jit(solution)/shard_map/all_to_all | solution.py:124
  150.1 1.3 copy.52
  151.5 1.1 constant_dynamic-slice_fusion
  152.5 4.3 %fusion = bf16[1024,256]{1,0:T(8,128)(2,1)} fusion(f32[1024,256]{1,0:T(8,128)S(1)} %bitcast.76, bf16[1024,2048]{1,0:T(8,128)(2,1)} %all-gather.5.cloned.1.call-done, bf16[256,2048]{1,0:T(8,128)(2,1)S(1)} %copy-done), kind=kOutput, calls=%fused_computation.4 | convolution fusion | flops 1074266112 | bytes 6815744 | tf_op jit(solution)/shard_map/dot_general | solution.py:103
  156.8 4.8 %reduce_sum.22 = bf16[1024,128]{1,0:T(8,128)(2,1)S(1)} reduce(bf16[32,1024,128]{2,1,0:T(8,128)(2,1)} %all-gather.3.cloned.1.call-done, bf16[]{:T(256)} %constant.38.clone.1), dimensions={0}, to_apply=%region_2.3 | reduce | flops 4063232 | bytes 8650754 | tf_op jit(solution)/shard_map/reduce_sum | solution.py:59
  162.1 0.8 reshape.83
  162.9 6.6 %all-to-all-start.3 = ((bf16[16,2,1024]{2,1,0:T(2,128)(2,1)}), bf16[16,2,1024]{2,1,0:T(2,128)(2,1)S(1)}, u32[]{:S(2)}, u32[]{:S(2)}) async-start(bf16[16,2,1024]{2,1,0:T(2,128)(2,1)} %reshape.83), calls=%async_computation.4 | async-start | bytes 131072 | tf_op jit(solution)/shard_map/all_to_all | solution.py:127
  169.8 87.5 %reduce-scatter.2.cloned.1.call-done = bf16[32,2048]{1,0:T(8,128)(2,1)} async-done(((bf16[1024,2048]{1,0:T(8,128)(2,1)}), bf16[32,2048]{1,0:T(8,128)(2,1)}) %reduce-scatter.2.cloned.1.call-update) | async-done | bytes 131088 | tf_op jit(solution)/shard_map/reduce_scatter | solution.py:60
  257.3 1.6 fusion.7
  259.4 0.8 fusion.17
  (42 shorter events, 3.7 us)
Async XLA Ops:
  7.2 49.0 %copy-start = (bf16[256,2048]{1,0:T(8,128)(2,1)S(1)}, bf16[256,2048]{1,0:T(8,128)(2,1)}, u32[]{:S(2)}) copy-start(bf16[256,2048]{1,0:T(8,128)(2,1)} %param.8) | copy-start | bytes 3145732
  7.2 47.9 %copy-start.1 = (bf16[1024,256]{1,0:T(8,128)(2,1)S(1)}, bf16[1024,256]{1,0:T(8,128)(2,1)}, u32[]{:S(2)}) copy-start(bf16[1024,256]{1,0:T(8,128)(2,1)} %param.7) | copy-start | bytes 1572868
  7.2 144.3 %all-gather.5.cloned.1.call-start = ((), (), s32[]{:S(2)}) async-start(), calls=%async_computation.7 | async-start | bytes 4325376 | tf_op jit(solution)/shard_map/all_gather | solution.py:99
  7.9 148.9 %all-gather.3.cloned.1.call-start = ((), (), s32[]{:S(2)}) async-start(), calls=%async_computation.6 | async-start | bytes 8650752 | tf_op jit(solution)/shard_map/all_gather | solution.py:58
  54.3 0.8 copy-start.2
  56.1 201.2 %reduce-scatter.2.cloned.1.call-start = ((), (), s32[]{:S(2)}) async-start(), calls=%async_computation.5 | async-start | bytes 4325376 | tf_op jit(solution)/shard_map/reduce_scatter | solution.py:60
  59.4 27.9 %copy-start.6 = (bf16[32,2048]{1,0:T(8,128)(2,1)S(1)}, bf16[32,2048]{1,0:T(8,128)(2,1)}, u32[]{:S(2)}) copy-start(bf16[32,2048]{1,0:T(8,128)(2,1)} %param.13) | copy-start | bytes 393220
  62.5 57.7 %copy-start.3 = (bf16[16,8,16,128]{3,2,0,1:T(8,128)(2,1)S(1)}, bf16[16,8,16,128]{3,2,0,1:T(8,128)(2,1)}, u32[]{:S(2)}) copy-start(bf16[16,8,16,128]{3,2,0,1:T(8,128)(2,1)} %copy-done.2) | copy-start | bytes 1572868
  87.3 0.7 copy-start.4
  114.4 35.1 %all-to-all-start.2 = ((bf16[8,256,128]{2,0,1:T(8,128)(2,1)}), bf16[8,256,128]{2,0,1:T(8,128)(2,1)S(1)}, u32[]{:S(2)}, u32[]{:S(2)}) async-start(bf16[8,256,128]{2,0,1:T(8,128)(2,1)} %copy.41), calls=%async_computation.3 | async-start | bytes 1048576 | tf_op jit(solution)/shard_map/all_to_all | solution.py:124
  156.8 12.7 %copy-start.5 = (bf16[64,2048]{1,0:T(8,128)(2,1)S(1)}, bf16[64,2048]{1,0:T(8,128)(2,1)}, u32[]{:S(2)}) copy-start(bf16[64,2048]{1,0:T(8,128)(2,1)} %copy-done.4) | copy-start | bytes 786436
  162.9 96.0 %all-to-all-start.3 = ((bf16[16,2,1024]{2,1,0:T(2,128)(2,1)}), bf16[16,2,1024]{2,1,0:T(2,128)(2,1)S(1)}, u32[]{:S(2)}, u32[]{:S(2)}) async-start(bf16[16,2,1024]{2,1,0:T(2,128)(2,1)} %reshape.83), calls=%async_computation.4 | async-start | bytes 131072 | tf_op jit(solution)/shard_map/all_to_all | solution.py:127
Sparse Core Ops, SparseCore 0:
  11.1 65.4 all-gather.4
  79.8 68.0 all-gather.2
  152.4 104.8 reduce-scatter.1
